TPU v7x, 32 devices: a whole 2x2x4 slice. The times are simulated.
32 devices in a mesh: gx: 4 (over z), gy: 8 (over y, x, core).
Axes of the slice: x: 2, y: 2, z: 4, core: 2. Of those that a mesh axis runs over, the one named last changes fastest.
Arguments:
- blocks: bfloat16 [256, 8, 256, 256], P(('gx', 'gy')), may hold values from -0.1875 to 0.1875
- block_cols: int32 [256, 8], P(('gx', 'gy')), may hold values from 0 to 23, as said below
- live_blocks: int32 [256], P(('gx', 'gy')), may hold values from 1 to 8
- send_rows: int32 [32, 4, 4], P(('gx', 'gy')), may hold values from 0 to 7, as said below
- start: float32 [256, 64, 256], P(('gx', 'gy')), may hold values from -6 to 6
- sketch: float32 [64, 256, 256], P(None, ('gx', 'gy')), may hold values from -0.0029296875 to 0.0029296875
Outputs:
- basis: float32 [4, 256, 64, 256], P(None, ('gx', 'gy'))
- factor: float32 [4, 4, 64], replicated
Inputs may be any that keep to these rules, and one draw needn't show every extreme that they name: block_cols[i, 0] is block row i itself (i % 8 in the owner's numbering); only the first live_blocks[i] entries of a row are used. `send_rows`: the 4 entries of one device and direction are distinct.
All inputs are finite; a program needn't handle non-finite values.
Results may differ from a plain program's by a relative error of at most 0.0036.
Values may be sent and summed in bfloat16 or wider, within the bound.
A program may use at most 64 MiB of HBM per device.

v0:
```python
import jax
import jax.numpy as jnp
from jax import lax
from jax.sharding import PartitionSpec as P

STEPS = 3


def with_halo(block, sides, width):
    for axis, dim in sides:
        count = lax.axis_size(axis)
        forward = [(i, i + 1) for i in range(count - 1)]
        forward.append((count - 1, 0))
        backward = [(target, source) for source, target in forward]
        low = lax.ppermute(
            lax.slice_in_dim(block, block.shape[dim] - width, None, axis=dim), axis, forward
        )
        high = lax.ppermute(lax.slice_in_dim(block, 0, width, axis=dim), axis, backward)
        block = jnp.concatenate([low, block, high], axis=dim)
    return block


def orthogonalize(sketched):
    count = sketched.shape[0]
    columns = []
    factor = jnp.zeros((count, count, sketched.shape[2]), jnp.float32)
    for column in range(count):
        residue = sketched[column]
        for earlier in range(column):
            coefficient = jnp.sum(columns[earlier] * sketched[column], axis=0)
            factor = factor.at[earlier, column].set(coefficient)
            residue = residue - coefficient[None, :] * columns[earlier]
        length = jnp.sqrt(jnp.sum(residue * residue, axis=0) + 1e-06)
        factor = factor.at[column, column].set(length)
        columns.append(residue / length[None, :])
    return factor


def sketch_local(sketch, vectors):
    return jnp.einsum("sib,irb->sr", sketch, vectors, precision=lax.Precision.HIGHEST)


def on_device(blocks, block_cols, live_blocks, send_rows, start, sketch):
    lists = send_rows[0]
    send_count = lists.shape[1]
    slot_count = block_cols.shape[1]
    weights = (jnp.arange(slot_count, dtype=jnp.int32)[None, :] < live_blocks[:, None]).astype(
        jnp.bfloat16
    )
    vectors = [start]
    for section in range(STEPS):
        rounded = vectors[-1].astype(jnp.bfloat16)
        outgoing_y = jnp.concatenate([rounded[lists[1]], rounded[lists[0]]], axis=0)
        outgoing_x = jnp.concatenate([rounded[lists[3]], rounded[lists[2]]], axis=0)
        around_y = with_halo(outgoing_y, (("gy", 0),), send_count)
        around_x = with_halo(outgoing_x, (("gx", 0),), send_count)
        from_left_y = around_y[:send_count]
        from_right_y = around_y[3 * send_count :]
        from_left_x = around_x[:send_count]
        from_right_x = around_x[3 * send_count :]
        extended = jnp.concatenate(
            [rounded, from_left_y, from_right_y, from_left_x, from_right_x], axis=0
        )
        picked = extended[block_cols] * weights[:, :, None, None]
        product = jnp.einsum("ikrb,ikbc->irc", picked, blocks, preferred_element_type=jnp.float32)
        vectors.append(product)
    partial_sketch = jnp.stack([sketch_local(sketch, vector) for vector in vectors])
    sketched = lax.psum(partial_sketch, ("gx", "gy"))
    factor = orthogonalize(sketched)
    result = []
    for column in range(STEPS + 1):
        accum = vectors[column]
        for earlier in range(column):
            accum = accum - factor[earlier, column][None, :, None] * result[earlier]
        result.append(accum / factor[column, column][None, :, None])
    return (jnp.stack(result), factor)


def solution(mesh):
    in_specs = (
        P(("gx", "gy"), None, None, None),
        P(("gx", "gy"), None),
        P(("gx", "gy")),
        P(("gx", "gy"), None, None),
        P(("gx", "gy"), None, None),
        P(None, ("gx", "gy"), None),
    )
    out_specs = (P(None, ("gx", "gy"), None, None), P())
    return jax.shard_map(
        on_device, mesh=mesh, in_specs=in_specs, out_specs=out_specs, check_vma=False
    )
```

profile of v0, /device:TPU:0, one launch (start us, length us, event | category | flops | bytes accessed | tf_op | source)
XLA Modules:
  0.0 223.7 jit_solution(15350976940218546734)
XLA Ops:
  7.2 0.0 all-reduce.3.cloned.1.call-start
  7.3 0.8 fusion.27
  8.1 1.1 constant_dynamic-update-slice_fusion.4
  9.2 0.6 gather_fusion
  9.8 0.5 collective-permute-start
  10.3 0.6 gather_fusion.1
  10.9 2.9 %collective-permute-start.1 = (bf16[4,64,256]{2,1,0:T(8,128)(2,1)S(1)}, bf16[4,64,256]{2,1,0:T(8,128)(2,1)S(1)}, u32[]{:S(2)}, u32[]{:S(2)}) collective-permute-start(bf16[4,64,256]{2,1,0:T(8,128)(2,1)S(1)} %gather_fusion.1), channel_id=1, source_target_pairs={{1,0},{2,1},{3,2},{4,3},{5,4},{6,5},{7,6},{0,7},{9,8},{10,9},{11,1... | collective-permute-start | bytes 393224 | tf_op jit(solution)/shard_map/ppermute | solution.py:18
  13.8 0.6 gather_fusion.2
  14.4 2.4 %collective-permute-start.2 = (bf16[4,64,256]{2,1,0:T(8,128)(2,1)S(1)}, bf16[4,64,256]{2,1,0:T(8,128)(2,1)S(1)}, u32[]{:S(2)}, u32[]{:S(2)}) collective-permute-start(bf16[4,64,256]{2,1,0:T(8,128)(2,1)S(1)} %gather_fusion.2), channel_id=1, source_target_pairs={{0,8},{8,16},{16,24},{24,0},{1,9},{9,17},{17,25},{25,1},{2,10},{10... | collective-permute-start | bytes 393224 | tf_op jit(solution)/shard_map/ppermute | solution.py:15
  16.8 0.6 gather_fusion.3
  17.3 2.1 collective-permute-start.3
  19.5 0.1 fusion.23
  19.5 0.7 convolution_bitcast_fusion.3
  20.2 0.6 fusion.36
  20.8 0.8 and_reduce_fusion
  21.6 0.6 fusion.35
  22.2 0.1 reshape.576
  22.4 0.4 collective-permute-done.2
  22.8 1.5 collective-permute-done.3
  24.3 0.7 gather_fusion.4
  24.9 5.9 %constant_dynamic-update-slice_fusion.9 = (bf16[24,64,256]{2,1,0:T(8,128)(2,1)S(1)}, bf16[8,64,256]{2,1,0:T(8,128)(2,1)}, f32[8,64,256]{2,1,0:T(8,128)}) fusion(bf16[8,8,256,256]{3,2,1,0:T(8,128)(2,1)} %param.26, bf16[8,8,64,256]{3,2,1,0:T(8,128)(2,1)S(1)} %bitcast.166, bf16[8,8]{1,0:T(8,128)(2,1)S(1)} %fusion.23), kind=kOutput, calls=%fused_computation.67 | convolution fusion | flops 538050560 | bytes 11534464 | tf_op jit(solution)/shard_map/ikrb,ikbc->irc/dot_general | solution.py:65
  30.8 1.5 gather_fusion.5
  32.3 1.5 gather_fusion.6
  33.8 1.5 gather_fusion.7
  35.3 1.5 gather_fusion.8
  36.9 0.1 collective-permute-start.4
  36.9 2.6 %collective-permute-start.5 = (bf16[4,64,256]{2,1,0:T(8,128)(2,1)S(1)}, bf16[4,64,256]{2,1,0:T(8,128)(2,1)S(1)}, u32[]{:S(2)}, u32[]{:S(2)}) collective-permute-start(bf16[4,64,256]{2,1,0:T(8,128)(2,1)S(1)} %gather_fusion.6), channel_id=1, source_target_pairs={{1,0},{2,1},{3,2},{4,3},{5,4},{6,5},{7,6},{0,7},{9,8},{10,9},{11,1... | collective-permute-start | bytes 393224 | tf_op jit(solution)/shard_map/ppermute | solution.py:18
  39.6 0.6 collective-permute-start.6
  40.1 3.3 %collective-permute-start.7 = (bf16[4,64,256]{2,1,0:T(8,128)(2,1)S(1)}, bf16[4,64,256]{2,1,0:T(8,128)(2,1)S(1)}, u32[]{:S(2)}, u32[]{:S(2)}) collective-permute-start(bf16[4,64,256]{2,1,0:T(8,128)(2,1)S(1)} %gather_fusion.8), channel_id=1, source_target_pairs={{8,0},{16,8},{24,16},{0,24},{9,1},{17,9},{25,17},{1,25},{10,2},{18... | collective-permute-start | bytes 393224 | tf_op jit(solution)/shard_map/ppermute | solution.py:18
  43.4 1.7 convolution_bitcast_fusion.2
  45.1 2.1 collective-permute-done.6
  47.3 0.7 gather_fusion.9
  48.0 5.9 %constant_dynamic-update-slice_fusion.14 = (bf16[24,64,256]{2,1,0:T(8,128)(2,1)S(1)}, bf16[8,64,256]{2,1,0:T(8,128)(2,1)}, f32[8,64,256]{2,1,0:T(8,128)}) fusion(bf16[8,8,256,256]{3,2,1,0:T(8,128)(2,1)} %param.26, bf16[8,8,64,256]{3,2,1,0:T(8,128)(2,1)S(1)} %bitcast.167, bf16[8,8]{1,0:T(8,128)(2,1)S(1)} %fusion.23), kind=kOutput, calls=%fused_computation.72 | convolution fusion | flops 538050560 | bytes 11534464 | tf_op jit(solution)/shard_map/ikrb,ikbc->irc/dot_general | solution.py:65
  53.9 1.5 gather_fusion.10
  55.4 1.5 gather_fusion.11
  56.9 1.5 gather_fusion.12
  58.4 1.5 gather_fusion.13
  59.9 0.1 collective-permute-start.8
  60.0 2.6 %collective-permute-start.9 = (bf16[4,64,256]{2,1,0:T(8,128)(2,1)S(1)}, bf16[4,64,256]{2,1,0:T(8,128)(2,1)S(1)}, u32[]{:S(2)}, u32[]{:S(2)}) collective-permute-start(bf16[4,64,256]{2,1,0:T(8,128)(2,1)S(1)} %gather_fusion.11), channel_id=1, source_target_pairs={{1,0},{2,1},{3,2},{4,3},{5,4},{6,5},{7,6},{0,7},{9,8},{10,9},{11,1... | collective-permute-start | bytes 393224 | tf_op jit(solution)/shard_map/ppermute | solution.py:18
  62.6 0.5 collective-permute-start.10
  63.2 3.3 %collective-permute-start.11 = (bf16[4,64,256]{2,1,0:T(8,128)(2,1)S(1)}, bf16[4,64,256]{2,1,0:T(8,128)(2,1)S(1)}, u32[]{:S(2)}, u32[]{:S(2)}) collective-permute-start(bf16[4,64,256]{2,1,0:T(8,128)(2,1)S(1)} %gather_fusion.13), channel_id=1, source_target_pairs={{8,0},{16,8},{24,16},{0,24},{9,1},{17,9},{25,17},{1,25},{10,2},{18... | collective-permute-start | bytes 393224 | tf_op jit(solution)/shard_map/ppermute | solution.py:18
  66.5 1.7 convolution_bitcast_fusion.1
  68.2 1.8 collective-permute-done.10
  70.0 0.5 collective-permute-done.11
  70.6 0.7 gather_fusion.14
  71.3 5.0 %fusion.12 = f32[8,64,256]{2,1,0:T(8,128)S(1)} fusion(bf16[8,8,256,256]{3,2,1,0:T(8,128)(2,1)} %param.26, bf16[8,8,64,256]{3,2,1,0:T(8,128)(2,1)S(1)} %bitcast.165, bf16[8,8]{1,0:T(8,128)(2,1)S(1)} %fusion.23), kind=kOutput, calls=%fused_computation.24 | convolution fusion | flops 537919488 | bytes 11010176 | tf_op jit(solution)/shard_map/ikrb,ikbc->irc/dot_general | solution.py:65
  76.3 0.7 convolution_bitcast_fusion
  77.0 0.7 pad_maximum_fusion.1
  77.7 0.6 fusion.37
  78.3 122.9 %all-reduce.3.cloned.1.call-done = f32[4,64,64]{2,1,0:T(8,128)} async-done(((f32[4,64,64]{2,1,0:T(8,128)}), f32[4,64,64]{2,1,0:T(8,128)}) %all-reduce.3.cloned.1.call-update) | async-done | bytes 65552 | tf_op jit(solution)/shard_map/psum | solution.py:68
  201.2 0.8 multiply_reduce_fusion.9
  202.0 0.8 multiply_reduce_fusion.8
  202.8 0.8 multiply_reduce_fusion.3
  203.6 0.8 multiply_reduce_fusion.2
  204.5 0.8 multiply_reduce_fusion.4
  205.3 0.8 multiply_reduce_fusion.1
  206.1 0.8 multiply_reduce_fusion
  207.0 1.3 scatter.35
  208.3 1.9 broadcast_select_fusion.1
  210.2 1.3 scatter.39
  211.6 1.8 broadcast_select_fusion
  213.4 1.3 scatter.44
  214.9 0.5 fusion.32
  215.4 1.5 pad_maximum_fusion
  (58 shorter events, 0.5 us)
Async XLA Ops:
  7.2 13.6 %copy-start.8 = (s32[3]{0:T(128)S(1)}, s32[3]{0:T(128)}, u32[]{:S(2)}) copy-start(s32[3]{0:T(128)} %constant.296.clone.1) | copy-start | bytes 40
  7.2 12.4 %copy-start.1 = (f32[8,64,256]{2,1,0:T(8,128)S(1)}, f32[8,64,256]{2,1,0:T(8,128)}, u32[]{:S(2)}) copy-start(f32[8,64,256]{2,1,0:T(8,128)} %param.30) | copy-start | bytes 1572868
  7.2 12.2 %copy-start.6 = (s32[8,8]{1,0:T(8,128)S(1)}, s32[8,8]{1,0:T(8,128)}, u32[]{:S(2)}) copy-start(s32[8,8]{1,0:T(8,128)} %param.27) | copy-start | bytes 772
  7.2 12.2 %copy-start.7 = (s32[8]{0:T(128)S(1)}, s32[8]{0:T(128)}, u32[]{:S(2)}) copy-start(s32[8]{0:T(128)} %param.28) | copy-start | bytes 100
  7.2 12.3 %copy-start = (f32[64,8,256]{2,1,0:T(8,128)S(1)}, f32[64,8,256]{2,1,0:T(8,128)}, u32[]{:S(2)}) copy-start(f32[64,8,256]{2,1,0:T(8,128)} %param.31) | copy-start | bytes 1572868
  7.2 193.9 %all-reduce.3.cloned.1.call-start = ((), (), s32[]{:S(2)}) async-start(), calls=%async_computation | async-start | bytes 262144 | tf_op jit(solution)/shard_map/psum | solution.py:68
  9.8 12.5 %collective-permute-start = (bf16[4,64,256]{2,1,0:T(8,128)(2,1)S(1)}, bf16[4,64,256]{2,1,0:T(8,128)(2,1)S(1)}, u32[]{:S(2)}, u32[]{:S(2)}) collective-permute-start(bf16[4,64,256]{2,1,0:T(8,128)(2,1)S(1)} %gather_fusion), channel_id=1, source_target_pairs={{0,1},{1,2},{2,3},{3,4},{4,5},{5,6},{6,7},{7,0},{8,9},{9,10},{10,1... | collective-permute-start | bytes 393224 | tf_op jit(solution)/shard_map/ppermute | solution.py:15
  10.9 11.5 %collective-permute-start.1 = (bf16[4,64,256]{2,1,0:T(8,128)(2,1)S(1)}, bf16[4,64,256]{2,1,0:T(8,128)(2,1)S(1)}, u32[]{:S(2)}, u32[]{:S(2)}) collective-permute-start(bf16[4,64,256]{2,1,0:T(8,128)(2,1)S(1)} %gather_fusion.1), channel_id=1, source_target_pairs={{1,0},{2,1},{3,2},{4,3},{5,4},{6,5},{7,6},{0,7},{9,8},{10,9},{11,1... | collective-permute-start | bytes 393224 | tf_op jit(solution)/shard_map/ppermute | solution.py:18
  14.4 8.4 %collective-permute-start.2 = (bf16[4,64,256]{2,1,0:T(8,128)(2,1)S(1)}, bf16[4,64,256]{2,1,0:T(8,128)(2,1)S(1)}, u32[]{:S(2)}, u32[]{:S(2)}) collective-permute-start(bf16[4,64,256]{2,1,0:T(8,128)(2,1)S(1)} %gather_fusion.2), channel_id=1, source_target_pairs={{0,8},{8,16},{16,24},{24,0},{1,9},{9,17},{17,25},{25,1},{2,10},{10... | collective-permute-start | bytes 393224 | tf_op jit(solution)/shard_map/ppermute | solution.py:15
  17.3 6.9 %collective-permute-start.3 = (bf16[4,64,256]{2,1,0:T(8,128)(2,1)S(1)}, bf16[4,64,256]{2,1,0:T(8,128)(2,1)S(1)}, u32[]{:S(2)}, u32[]{:S(2)}) collective-permute-start(bf16[4,64,256]{2,1,0:T(8,128)(2,1)S(1)} %gather_fusion.3), channel_id=1, source_target_pairs={{8,0},{16,8},{24,16},{0,24},{9,1},{17,9},{25,17},{1,25},{10,2},{18... | collective-permute-start | bytes 393224 | tf_op jit(solution)/shard_map/ppermute | solution.py:18
  36.9 8.2 %collective-permute-start.4 = (bf16[4,64,256]{2,1,0:T(8,128)(2,1)S(1)}, bf16[4,64,256]{2,1,0:T(8,128)(2,1)S(1)}, u32[]{:S(2)}, u32[]{:S(2)}) collective-permute-start(bf16[4,64,256]{2,1,0:T(8,128)(2,1)S(1)} %gather_fusion.5), channel_id=1, source_target_pairs={{0,1},{1,2},{2,3},{3,4},{4,5},{5,6},{6,7},{7,0},{8,9},{9,10},{10,1... | collective-permute-start | bytes 393224 | tf_op jit(solution)/shard_map/ppermute | solution.py:15
  36.9 8.2 %collective-permute-start.5 = (bf16[4,64,256]{2,1,0:T(8,128)(2,1)S(1)}, bf16[4,64,256]{2,1,0:T(8,128)(2,1)S(1)}, u32[]{:S(2)}, u32[]{:S(2)}) collective-permute-start(bf16[4,64,256]{2,1,0:T(8,128)(2,1)S(1)} %gather_fusion.6), channel_id=1, source_target_pairs={{1,0},{2,1},{3,2},{4,3},{5,4},{6,5},{7,6},{0,7},{9,8},{10,9},{11,1... | collective-permute-start | bytes 393224 | tf_op jit(solution)/shard_map/ppermute | solution.py:18
  39.6 7.7 %collective-permute-start.6 = (bf16[4,64,256]{2,1,0:T(8,128)(2,1)S(1)}, bf16[4,64,256]{2,1,0:T(8,128)(2,1)S(1)}, u32[]{:S(2)}, u32[]{:S(2)}) collective-permute-start(bf16[4,64,256]{2,1,0:T(8,128)(2,1)S(1)} %gather_fusion.7), channel_id=1, source_target_pairs={{0,8},{8,16},{16,24},{24,0},{1,9},{9,17},{17,25},{25,1},{2,10},{10... | collective-permute-start | bytes 393224 | tf_op jit(solution)/shard_map/ppermute | solution.py:15
  40.1 7.2 %collective-permute-start.7 = (bf16[4,64,256]{2,1,0:T(8,128)(2,1)S(1)}, bf16[4,64,256]{2,1,0:T(8,128)(2,1)S(1)}, u32[]{:S(2)}, u32[]{:S(2)}) collective-permute-start(bf16[4,64,256]{2,1,0:T(8,128)(2,1)S(1)} %gather_fusion.8), channel_id=1, source_target_pairs={{8,0},{16,8},{24,16},{0,24},{9,1},{17,9},{25,17},{1,25},{10,2},{18... | collective-permute-start | bytes 393224 | tf_op jit(solution)/shard_map/ppermute | solution.py:18
  59.9 8.2 %collective-permute-start.8 = (bf16[4,64,256]{2,1,0:T(8,128)(2,1)S(1)}, bf16[4,64,256]{2,1,0:T(8,128)(2,1)S(1)}, u32[]{:S(2)}, u32[]{:S(2)}) collective-permute-start(bf16[4,64,256]{2,1,0:T(8,128)(2,1)S(1)} %gather_fusion.10), channel_id=1, source_target_pairs={{0,1},{1,2},{2,3},{3,4},{4,5},{5,6},{6,7},{7,0},{8,9},{9,10},{10,1... | collective-permute-start | bytes 393224 | tf_op jit(solution)/shard_map/ppermute | solution.py:15
  60.0 8.2 %collective-permute-start.9 = (bf16[4,64,256]{2,1,0:T(8,128)(2,1)S(1)}, bf16[4,64,256]{2,1,0:T(8,128)(2,1)S(1)}, u32[]{:S(2)}, u32[]{:S(2)}) collective-permute-start(bf16[4,64,256]{2,1,0:T(8,128)(2,1)S(1)} %gather_fusion.11), channel_id=1, source_target_pairs={{1,0},{2,1},{3,2},{4,3},{5,4},{6,5},{7,6},{0,7},{9,8},{10,9},{11,1... | collective-permute-start | bytes 393224 | tf_op jit(solution)/shard_map/ppermute | solution.py:18
  62.6 7.4 %collective-permute-start.10 = (bf16[4,64,256]{2,1,0:T(8,128)(2,1)S(1)}, bf16[4,64,256]{2,1,0:T(8,128)(2,1)S(1)}, u32[]{:S(2)}, u32[]{:S(2)}) collective-permute-start(bf16[4,64,256]{2,1,0:T(8,128)(2,1)S(1)} %gather_fusion.12), channel_id=1, source_target_pairs={{0,8},{8,16},{16,24},{24,0},{1,9},{9,17},{17,25},{25,1},{2,10},{10... | collective-permute-start | bytes 393224 | tf_op jit(solution)/shard_map/ppermute | solution.py:15
  63.2 7.4 %collective-permute-start.11 = (bf16[4,64,256]{2,1,0:T(8,128)(2,1)S(1)}, bf16[4,64,256]{2,1,0:T(8,128)(2,1)S(1)}, u32[]{:S(2)}, u32[]{:S(2)}) collective-permute-start(bf16[4,64,256]{2,1,0:T(8,128)(2,1)S(1)} %gather_fusion.13), channel_id=1, source_target_pairs={{8,0},{16,8},{24,16},{0,24},{9,1},{17,9},{25,17},{1,25},{10,2},{18... | collective-permute-start | bytes 393224 | tf_op jit(solution)/shard_map/ppermute | solution.py:18
  76.3 138.6 %copy-start.2 = (f32[8,64,256]{2,1,0:T(8,128)S(1)}, f32[8,64,256]{2,1,0:T(8,128)}, u32[]{:S(2)}) copy-start(f32[8,64,256]{2,1,0:T(8,128)} %param.30) | copy-start | bytes 1572868
  76.3 138.6 %copy-start.3 = (f32[8,64,256]{2,1,0:T(8,128)S(1)}, f32[8,64,256]{2,1,0:T(8,128)}, u32[]{:S(2)}) copy-start(f32[8,64,256]{2,1,0:T(8,128)} %get-tuple-element.168) | copy-start | bytes 1572868
  76.3 138.6 %copy-start.4 = (f32[8,64,256]{2,1,0:T(8,128)S(1)}, f32[8,64,256]{2,1,0:T(8,128)}, u32[]{:S(2)}) copy-start(f32[8,64,256]{2,1,0:T(8,128)} %get-tuple-element.169) | copy-start | bytes 1572868
  214.8 0.6 copy-start.5
Sparse Core Ops, SparseCore 0:
  77.8 123.3 all-reduce.2
where the time goes:
time: 225 us; the launch traced here: 224 us
  waiting for transfers between devices  129 us (57%)
  local copies, waits for them, and re-layouts  22.5 us (10%)
  matrix products  21.4 us (10%)
  starting transfers between devices  21 us (9%)
  other arithmetic  15 us (7%)
  between operations  14.5 us (6%)
    psum x1, waiting for transfers between devices, on_device(): sketched = lax.psum(partial_sketch, ('gx', 'gy'))  123 us
    ppermute x6, starting transfers between devices, with_halo(): lax.ppermute(lax.slice_in_dim(block, 0, width, axis=dim), axis, backward)  16.9 us
    dot_general x3, matrix products, on_device(): jnp.einsum('ikrb,ikbc->irc', picked, blocks, preferred_element_type=jnp.f...  16.7 us
    gather x6, local copies, waits for them, and re-layouts, on_device(): outgoing_x = jnp.concatenate([rounded[lists[3]], rounded[lists[2]]], axis=0)  7.13 us
    gather x6, local copies, waits for them, and re-layouts, on_device(): outgoing_y = jnp.concatenate([rounded[lists[1]], rounded[lists[0]]], axis=0)  7.12 us
    dot_general x4, matrix products, sketch_local(): jnp.einsum('sib,irb->sr', sketch, vectors, precision=lax.Precision.HIGHEST)  4.69 us
    another operation x4, other arithmetic  4.55 us
  transfers between devices with their start and end apart: 13, of which 6 were waited for; matrix products, arithmetic and copies ran while one was open for 4% of the time, Pallas kernels for 0%

commit v1 on v0

v1 whole, which is shorter than its diff:
```python
import functools

import jax
import jax.numpy as jnp
from jax import lax
from jax.experimental import pallas as pl
from jax.experimental.pallas import tpu as pltpu
from jax.sharding import PartitionSpec as P

STEPS = 3
MESH = pl.DeviceIdType.MESH
F32 = jnp.float32
BF16 = jnp.bfloat16


def contract_last(a, b):
    return lax.dot_general(a, b, (((1,), (1,)), ((), ())), preferred_element_type=F32)


def split_bf16(x):
    high = x.astype(BF16)
    low = (x - high.astype(F32)).astype(BF16)
    return high, low


def power_kernel(
    ngx,
    ngy,
    cols_hbm,
    live_hbm,
    lists_hbm,
    blocks_hbm,
    start_hbm,
    sketch_hbm,
    vecs,
    fac_out,
    cols,
    live,
    lists,
    blk,
    v0,
    sk,
    shl,
    ext0,
    ext1,
    ext2,
    outgoing,
    wsend,
    wrecv,
    gxbuf,
    fbuf,
    sem_lists,
    sem_local,
    sem_blk,
    halo_s,
    halo_r,
    p1s,
    p1r,
    p2s,
    p2r,
    p3s,
    p3r,
):
    ext = (ext0, ext1, ext2)
    rows, rhs, width = v0.shape
    slots = cols.shape[1]
    send_count = lists.shape[1]
    sk_rows = shl.shape[1] // 2
    zero_slot = ext0.shape[0] - 1
    chunk = rhs // ngy
    g, h = lax.axis_index("gx"), lax.axis_index("gy")

    scalar_loads = [
        pltpu.make_async_copy(source, target, sem_lists.at[n])
        for n, (source, target) in enumerate(
            ((lists_hbm, lists), (cols_hbm, cols), (live_hbm, live))
        )
    ]
    for load in scalar_loads:
        load.start()
    load_start = pltpu.make_async_copy(start_hbm, v0, sem_local.at[0])
    load_start.start()
    parts_wide = sk.shape[0]

    def sketch_copy(c):
        return pltpu.make_async_copy(
            sketch_hbm.at[:, pl.ds(c * 128, 128)], sk.at[c], sem_local.at[1 + c]
        )

    for c in range(parts_wide):
        sketch_copy(c).start()

    def block_copy(i):
        return pltpu.make_async_copy(blocks_hbm.at[i], blk.at[i], sem_blk.at[i])

    for i in range(rows):
        block_copy(i).start()

    barrier = pltpu.get_barrier_semaphore()
    for delta in range(1, ngy):
        pl.semaphore_signal(
            barrier, inc=1, device_id={"gy": lax.rem(h + delta, ngy)}, device_id_type=MESH
        )
    for delta in range(1, ngx):
        pl.semaphore_signal(
            barrier, inc=1, device_id={"gx": lax.rem(g + delta, ngx)}, device_id_type=MESH
        )

    for s in range(STEPS):
        ext[s][zero_slot] = jnp.zeros((rhs, width), BF16)

    targets = (
        {"gy": lax.rem(h + 1, ngy)},
        {"gy": lax.rem(h + ngy - 1, ngy)},
        {"gx": lax.rem(g + 1, ngx)},
        {"gx": lax.rem(g + ngx - 1, ngx)},
    )
    order = (2, 3, 0, 1)

    def halo_copy(s, d):
        return pltpu.make_async_remote_copy(
            src_ref=outgoing.at[s, d],
            dst_ref=ext[s].at[pl.ds(rows + d * send_count, send_count)],
            send_sem=halo_s.at[s, d],
            recv_sem=halo_r.at[s, d],
            device_id=targets[d],
            device_id_type=MESH,
        )

    def gather_outgoing(s, d):
        for j in range(send_count):
            source = v0[lists[d, j]] if s == 0 else vecs[s - 1, lists[d, j]]
            outgoing[s, d, j] = source.astype(BF16)

    def p1_copy(s, delta):
        to = lax.rem(h + delta, ngy)
        return pltpu.make_async_remote_copy(
            src_ref=wsend.at[s, to],
            dst_ref=wrecv.at[s, delta - 1],
            send_sem=p1s.at[s, delta - 1],
            recv_sem=p1r.at[s, delta - 1],
            device_id={"gy": to},
            device_id_type=MESH,
        )

    def p2_copy(s, delta):
        return pltpu.make_async_remote_copy(
            src_ref=gxbuf.at[s, g],
            dst_ref=gxbuf.at[s, g],
            send_sem=p2s.at[s, delta - 1],
            recv_sem=p2r.at[s, delta - 1],
            device_id={"gx": lax.rem(g + delta, ngx)},
            device_id_type=MESH,
        )

    def p3_copy(delta):
        return pltpu.make_async_remote_copy(
            src_ref=fbuf.at[h],
            dst_ref=fbuf.at[h],
            send_sem=p3s.at[delta - 1],
            recv_sem=p3r.at[delta - 1],
            device_id={"gy": lax.rem(h + delta, ngy)},
            device_id_type=MESH,
        )

    def sketch_of(s):
        total = jnp.zeros((2 * rhs, 2 * sk_rows), F32)
        for i in range(rows):
            value = v0[i] if s == 0 else vecs[s - 1, i]
            high, low = split_bf16(value)
            total = total + contract_last(jnp.concatenate([high, low], axis=0), shl[i])
        total = total[:rhs] + total[rhs:]
        for c in range(ngy):
            wsend[s, c] = total[c * chunk : (c + 1) * chunk]
        for delta in range(1, ngy):
            p1_copy(s, delta).start()

    def finish_gy(s):
        total = wsend[s, h]
        for delta in range(1, ngy):
            p1_copy(s, delta).wait_recv()
            total = total + wrecv[s, delta - 1]
        gxbuf[s, g] = total
        for delta in range(1, ngx):
            p2_copy(s, delta).start()

    units = []
    state = {"fac": jnp.zeros((chunk, 128), F32)}
    lane = lax.broadcasted_iota(jnp.int32, (chunk, 128), 1)

    def put(row, column, value):
        state["fac"] = jnp.where(lane == row * (STEPS + 1) + column, value, state["fac"])

    def finish_gx(s):
        for delta in range(1, ngx):
            p2_copy(s, delta).wait_recv()
        total = gxbuf[s, 0]
        for other in range(1, ngx):
            total = total + gxbuf[s, other]
        w = total[:, :sk_rows] + total[:, sk_rows:]
        residue = w
        for m in range(s):
            coefficient = jnp.sum(units[m] * w, axis=1, keepdims=True)
            put(m, s, coefficient)
            residue = residue - coefficient * units[m]
        length = jnp.sqrt(jnp.sum(residue * residue, axis=1, keepdims=True) + 1e-06)
        put(s, s, length)
        units.append(residue / length)

    for load in scalar_loads:
        load.wait()
    load_start.wait()
    for d in order:
        gather_outgoing(0, d)
    pl.semaphore_wait(barrier, ngx + ngy - 2)
    for d in order:
        halo_copy(0, d).start()
    for i in range(rows):
        ext[0][i] = v0[i].astype(BF16)

    for c in range(parts_wide):
        sketch_copy(c).wait()
        for i in range(rows):
            high, low = split_bf16(sk[c, pl.ds(i, sk_rows, stride=rows), :])
            shl[i, :, c * 128 : (c + 1) * 128] = jnp.concatenate([high, low], axis=0)
    sketch_of(0)

    for s in range(STEPS):
        for d in order:
            halo_copy(s, d).wait_recv()

        def row(i, carry):
            if s == 0:
                block_copy(i).wait()
            parts = [ext[s][i]]
            for k in range(1, slots):
                parts.append(ext[s][jnp.where(k < live[i], cols[i, k], zero_slot)])
            product = jnp.dot(
                jnp.concatenate(parts, axis=1), blk[i], preferred_element_type=F32
            )
            vecs[s, i] = product
            if s + 1 < STEPS:
                ext[s + 1][i] = product.astype(BF16)
            return carry

        lax.fori_loop(0, rows, row, 0)
        if s + 1 < STEPS:
            for d in order:
                gather_outgoing(s + 1, d)
                halo_copy(s + 1, d).start()
        sketch_of(s + 1)
        finish_gy(s)
        if s > 0:
            finish_gx(s - 1)

    finish_gx(STEPS - 1)
    finish_gy(STEPS)
    finish_gx(STEPS)
    fbuf[h] = state["fac"]
    for delta in range(1, ngy):
        p3_copy(delta).start()
    for delta in range(1, ngy):
        p3_copy(delta).wait_recv()
    for c in range(ngy):
        fac_out[c * chunk : (c + 1) * chunk, :] = fbuf[c]

    for s in range(STEPS):
        for d in order:
            halo_copy(s, d).wait_send()
    for s in range(STEPS + 1):
        for delta in range(1, ngy):
            p1_copy(s, delta).wait_send()
        for delta in range(1, ngx):
            p2_copy(s, delta).wait_send()
    for delta in range(1, ngy):
        p3_copy(delta).wait_send()


def basis_kernel(start, vecs, fac, basis_hbm, factor, result, sem):
    rows, rhs, width = start.shape
    count = STEPS + 1
    lanes = fac[...].T
    for m in range(count):
        factor[m] = lanes[m * count : (m + 1) * count, :]
    group = 8

    def out_copy(c):
        part = pl.ds(pl.multiple_of(c * group, group), group)
        return pltpu.make_async_copy(
            result.at[:, :, part, :], basis_hbm.at[:, :, part, :], sem.at[c]
        )

    def body(c, carry):
        part = pl.ds(pl.multiple_of(c * group, group), group)
        f = fac[part, :]

        def spread(column):
            return jnp.broadcast_to(column, (group, width))

        upper = {
            (m, s): spread(f[:, m * count + s : m * count + s + 1])
            for s in range(count)
            for m in range(s)
        }
        inverse = [
            spread(1.0 / f[:, s * count + s : s * count + s + 1]) for s in range(count)
        ]
        for i in range(rows):
            done = []
            for s in range(count):
                value = start[i, part, :] if s == 0 else vecs[s - 1, i, part, :]
                for m in range(s):
                    value = value - upper[m, s] * done[m]
                value = value * inverse[s]
                done.append(value)
                result[s, i, part, :] = value
        out_copy(c).start()
        return carry

    lax.fori_loop(0, rhs // group, body, 0)
    for c in range(rhs // group):
        out_copy(c).wait()


def on_device(ngx, ngy, blocks, block_cols, live_blocks, send_rows, start, sketch):
    rows, slots, width, _ = blocks.shape
    rhs = start.shape[1]
    sk_rows = sketch.shape[0]
    directions, send_count = send_rows.shape[1:]
    chunk = rhs // ngy
    count = STEPS + 1
    places = rows + directions * send_count + 1
    hbm = pl.BlockSpec(memory_space=pltpu.HBM)
    vmem = pl.BlockSpec(memory_space=pltpu.VMEM)
    dma = pltpu.SemaphoreType.DMA
    vecs, fac = pl.pallas_call(
        functools.partial(power_kernel, ngx, ngy),
        name="power",
        out_shape=[
            jax.ShapeDtypeStruct((STEPS, rows, rhs, width), F32),
            jax.ShapeDtypeStruct((rhs, 128), F32),
        ],
        in_specs=[hbm] * 6,
        out_specs=[vmem, vmem],
        scratch_shapes=[
            pltpu.SMEM(block_cols.shape, jnp.int32),
            pltpu.SMEM(live_blocks.shape, jnp.int32),
            pltpu.SMEM(send_rows.shape[1:], jnp.int32),
            pltpu.VMEM((rows, slots * width, width), BF16),
            pltpu.VMEM((rows, rhs, width), F32),
            pltpu.VMEM((width // 128, sk_rows * rows, 128), F32),
            pltpu.VMEM((rows, 2 * sk_rows, width), BF16),
            *[pltpu.VMEM((places, rhs, width), BF16) for step in range(STEPS)],
            pltpu.VMEM((STEPS, directions, send_count, rhs, width), BF16),
            pltpu.VMEM((count, ngy, chunk, 2 * sk_rows), F32),
            pltpu.VMEM((count, ngy - 1, chunk, 2 * sk_rows), F32),
            pltpu.VMEM((count, ngx, chunk, 2 * sk_rows), F32),
            pltpu.VMEM((ngy, chunk, 128), F32),
            dma((3,)),
            dma((1 + width // 128,)),
            dma((rows,)),
            dma((STEPS, directions)),
            dma((STEPS, directions)),
            dma((count, ngy - 1)),
            dma((count, ngy - 1)),
            dma((count, ngx - 1)),
            dma((count, ngx - 1)),
            dma((ngy - 1,)),
            dma((ngy - 1,)),
        ],
        compiler_params=pltpu.CompilerParams(
            collective_id=0, has_side_effects=True, vmem_limit_bytes=40 * 1024 * 1024
        ),
    )(
        *(
            pltpu.with_memory_space_constraint(array, pltpu.HBM)
            for array in (
                block_cols,
                live_blocks,
                send_rows[0],
                blocks.reshape(rows, slots * width, width),
                start,
                sketch.reshape(sk_rows * rows, width),
            )
        )
    )
    basis, factor = pl.pallas_call(
        basis_kernel,
        name="basis",
        out_shape=[
            jax.ShapeDtypeStruct((count, rows, rhs, width), F32),
            jax.ShapeDtypeStruct((count, count, rhs), F32),
        ],
        in_specs=[vmem, vmem, vmem],
        out_specs=[hbm, vmem],
        scratch_shapes=[
            pltpu.VMEM((count, rows, rhs, width), F32),
            dma((rhs // 8,)),
        ],
        compiler_params=pltpu.CompilerParams(vmem_limit_bytes=16 * 1024 * 1024),
    )(start, vecs, fac)
    return basis, factor


def solution(mesh):
    in_specs = (
        P(("gx", "gy"), None, None, None),
        P(("gx", "gy"), None),
        P(("gx", "gy")),
        P(("gx", "gy"), None, None),
        P(("gx", "gy"), None, None),
        P(None, ("gx", "gy"), None),
    )
    out_specs = (P(None, ("gx", "gy"), None, None), P())
    return jax.shard_map(
        functools.partial(on_device, mesh.shape["gx"], mesh.shape["gy"]),
        mesh=mesh,
        in_specs=in_specs,
        out_specs=out_specs,
        check_vma=False,
    )
```

time: 225 us -> 51.4 us (0.23)
  waiting for transfers between devices: 129 us -> 0 us
  Pallas kernels: 0 us -> 50.6 us
  local copies, waits for them, and re-layouts: 22.5 us -> 0.01 us
  matrix products: 21.4 us -> 0 us
  starting transfers between devices: 21 us -> 0 us
  other arithmetic: 15 us -> 0 us
  between operations: 14.5 us -> 0.66 us
    psum x1 -> x0, waiting for transfers between devices: 123 us -> none  [on_device(): sketched = lax.psum(partial_sketch, ('gx', 'gy'))]
    pallas_call x0 -> x2, Pallas kernels: none -> 50.6 us  [the longest x1 48.2 us: on_device(): pl.pallas_call(functools.partial(power_kernel, ngx, ngy), name='power', o...]
    dot_general x7 -> x0, matrix products: 21.4 us -> none  [the longest x3 16.7 us: on_device(): jnp.einsum('ikrb,ikbc->irc', picked, blocks, preferred_element_type=jnp.f...]
    ppermute x12 -> x0, starting transfers between devices: 21 us -> none  [the longest x6 16.9 us: with_halo(): lax.ppermute(lax.slice_in_dim(block, 0, width, axis=dim), axis, backward)]
    gather x15 -> x0, local copies, waits for them, and re-layouts: 16.3 us -> none  [the longest x6 7.13 us: on_device(): outgoing_x = jnp.concatenate([rounded[lists[3]], rounded[lists[2]]], axis=0)]
    another operation x7 -> x0, other arithmetic: 7.19 us -> none
    ppermute x12 -> x0, waiting for transfers between devices: 6.36 us -> none  [the longest x6 4.34 us: with_halo(): lax.ppermute(lax.slice_in_dim(block, block.shape[dim] - width, None, axis...]
    reduce_sum x7 -> x0, other arithmetic: 5.73 us -> none  [the longest x4 3.29 us: orthogonalize(): coefficient = jnp.sum(columns[earlier] * sketched[column], axis=0)]
  transfers between devices with their start and end apart: 13 -> 0, of which waited for: 6 -> 0; matrix products, arithmetic and copies ran while one was open for 4% -> 0% of each run, Pallas kernels for 0% -> 0%
where the time goes in v1:
time: 51.4 us; the launch traced here: 51.2 us
  Pallas kernels  50.6 us (98%)
  between operations  0.66 us (1%)
    pallas_call x1, Pallas kernels, on_device(): pl.pallas_call(functools.partial(power_kernel, ngx, ngy), name='power', o...  48.2 us
    pallas_call x1, Pallas kernels, on_device(): pl.pallas_call(basis_kernel, name='basis', out_shape=[jax.ShapeDtypeStruc...  2.37 us

profile of v1, /device:TPU:0, one launch (start us, length us, event | category | flops | bytes accessed | tf_op | source)
XLA Modules:
  0.0 51.2 jit_solution(5740988490601707644)
XLA Ops:
  0.6 0.0 copy-start
  0.6 48.2 %power.1 = (f32[3,8,64,256]{3,2,1,0:T(8,128)S(1)}, f32[64,128]{1,0:T(8,128)S(1)}) custom-call(s32[8,8]{1,0:T(8,128)} %cols_hbm.1, s32[8]{0:T(128)} %live_hbm.1, s32[4,4]{1,0:T(4,128)} %bitcast.5, bf16[8,2048,256]{2,1,0:T(8,128)(2,1)} %bitcast.3, f32[8,64,256]{2,1,0:T(8,128)} %start.1, f32[512,256]{1,0:T(8,128)} %bitcast.4), custom_call_target="tpu_custom_call" | custom-call | tf_op jit(solution)/shard_map/power/pallas_call | solution.py:336
  48.9 0.0 copy-done
  48.9 2.4 %basis.1 = (f32[4,8,64,256]{3,2,1,0:T(8,128)}, f32[4,4,64]{2,1,0:T(4,128)}) custom-call(f32[8,64,256]{2,1,0:T(8,128)S(1)} %copy-done, f32[3,8,64,256]{3,2,1,0:T(8,128)S(1)} %get-tuple-element.4.vecs, f32[64,128]{1,0:T(8,128)S(1)} %get-tuple-element.5.fac), custom_call_target="tpu_custom_call" | custom-call | tf_op jit(solution)/shard_map/basis/pallas_call | solution.py:387
Async XLA Ops:
  0.6 48.2 %copy-start = (f32[8,64,256]{2,1,0:T(8,128)S(1)}, f32[8,64,256]{2,1,0:T(8,128)}, u32[]{:S(2)}) copy-start(f32[8,64,256]{2,1,0:T(8,128)} %start.1) | copy-start | bytes 1572868

commit v2 on v1

--- a/solution.py
+++ b/solution.py
@@ -8,6 +8,8 @@
 from jax.sharding import PartitionSpec as P
 
 STEPS = 3
+CHUNKS = 2
+UNROLL = 8
 MESH = pl.DeviceIdType.MESH
 F32 = jnp.float32
 BF16 = jnp.bfloat16
@@ -41,10 +43,8 @@
     v0,
     sk,
     shl,
-    ext0,
-    ext1,
-    ext2,
     outgoing,
+    kept,
     wsend,
     wrecv,
     gxbuf,
@@ -60,13 +60,15 @@
     p2r,
     p3s,
     p3r,
+    *halves,
 ):
-    ext = (ext0, ext1, ext2)
+    ext = [halves[s * CHUNKS : (s + 1) * CHUNKS] for s in range(STEPS)]
     rows, rhs, width = v0.shape
+    part = rhs // CHUNKS
     slots = cols.shape[1]
     send_count = lists.shape[1]
     sk_rows = shl.shape[1] // 2
-    zero_slot = ext0.shape[0] - 1
+    zero_slot = halves[0].shape[0] - 1
     chunk = rhs // ngy
     g, h = lax.axis_index("gx"), lax.axis_index("gy")
 
@@ -106,8 +108,8 @@
             barrier, inc=1, device_id={"gx": lax.rem(g + delta, ngx)}, device_id_type=MESH
         )
 
-    for s in range(STEPS):
-        ext[s][zero_slot] = jnp.zeros((rhs, width), BF16)
+    for half in halves:
+        half[zero_slot] = jnp.zeros((part, width), BF16)
 
     targets = (
         {"gy": lax.rem(h + 1, ngy)},
@@ -117,20 +119,26 @@
     )
     order = (2, 3, 0, 1)
 
-    def halo_copy(s, d):
+    def halo_copy(s, c, d):
         return pltpu.make_async_remote_copy(
-            src_ref=outgoing.at[s, d],
-            dst_ref=ext[s].at[pl.ds(rows + d * send_count, send_count)],
-            send_sem=halo_s.at[s, d],
-            recv_sem=halo_r.at[s, d],
+            src_ref=outgoing.at[s, c, d],
+            dst_ref=ext[s][c].at[pl.ds(rows + d * send_count, send_count)],
+            send_sem=halo_s.at[s, c, d],
+            recv_sem=halo_r.at[s, c, d],
             device_id=targets[d],
             device_id_type=MESH,
         )
 
-    def gather_outgoing(s, d):
+    def span(c):
+        return slice(c * part, (c + 1) * part)
+
+    def gather_outgoing(s, c, d):
         for j in range(send_count):
-            source = v0[lists[d, j]] if s == 0 else vecs[s - 1, lists[d, j]]
-            outgoing[s, d, j] = source.astype(BF16)
+            if s == 0:
+                source = v0[lists[d, j], span(c), :]
+            else:
+                source = vecs[s - 1, lists[d, j], span(c), :]
+            outgoing[s, c, d, j] = source.astype(BF16)
 
     def p1_copy(s, delta):
         to = lax.rem(h + delta, ngy)
@@ -163,17 +171,30 @@
             device_id_type=MESH,
         )
 
-    def sketch_of(s):
-        total = jnp.zeros((2 * rhs, 2 * sk_rows), F32)
+    sketched = {}
+
+    def sketch_of(s, c):
+        total = jnp.zeros((2 * part, 2 * sk_rows), F32)
         for i in range(rows):
-            value = v0[i] if s == 0 else vecs[s - 1, i]
+            value = v0[i, span(c), :] if s == 0 else vecs[s - 1, i, span(c), :]
             high, low = split_bf16(value)
             total = total + contract_last(jnp.concatenate([high, low], axis=0), shl[i])
-        total = total[:rhs] + total[rhs:]
-        for c in range(ngy):
-            wsend[s, c] = total[c * chunk : (c + 1) * chunk]
+        total = total[:part] + total[part:]
+        sketched[s, c] = total[:, :sk_rows] + total[:, sk_rows:]
+
+    def keep_first(pair):
+        for c in range(CHUNKS):
+            kept[pair, span(c), :] = sketched[2 * pair, c]
+
+    def send_pair(pair):
+        for c in range(CHUNKS):
+            both = jnp.concatenate(
+                [kept[pair, span(c), :], sketched[2 * pair + 1, c]], axis=1
+            )
+            for k in range(part // chunk):
+                wsend[pair, c * (part // chunk) + k] = both[k * chunk : (k + 1) * chunk]
         for delta in range(1, ngy):
-            p1_copy(s, delta).start()
+            p1_copy(pair, delta).start()
 
     def finish_gy(s):
         total = wsend[s, h]
@@ -191,71 +212,87 @@
     def put(row, column, value):
         state["fac"] = jnp.where(lane == row * (STEPS + 1) + column, value, state["fac"])
 
-    def finish_gx(s):
+    def finish_gx(pair):
         for delta in range(1, ngx):
-            p2_copy(s, delta).wait_recv()
-        total = gxbuf[s, 0]
+            p2_copy(pair, delta).wait_recv()
+        total = gxbuf[pair, 0]
         for other in range(1, ngx):
-            total = total + gxbuf[s, other]
-        w = total[:, :sk_rows] + total[:, sk_rows:]
-        residue = w
-        for m in range(s):
-            coefficient = jnp.sum(units[m] * w, axis=1, keepdims=True)
-            put(m, s, coefficient)
-            residue = residue - coefficient * units[m]
-        length = jnp.sqrt(jnp.sum(residue * residue, axis=1, keepdims=True) + 1e-06)
-        put(s, s, length)
-        units.append(residue / length)
+            total = total + gxbuf[pair, other]
+        for s in (2 * pair, 2 * pair + 1):
+            w = total[:, (s % 2) * sk_rows : (s % 2 + 1) * sk_rows]
+            residue = w
+            for m in range(s):
+                coefficient = jnp.sum(units[m] * w, axis=1, keepdims=True)
+                put(m, s, coefficient)
+                residue = residue - coefficient * units[m]
+            square = jnp.sum(residue * residue, axis=1, keepdims=True)
+            length = jnp.sqrt(square + 1e-06)
+            put(s, s, length)
+            units.append(residue / length)
 
     for load in scalar_loads:
         load.wait()
     load_start.wait()
-    for d in order:
-        gather_outgoing(0, d)
-    pl.semaphore_wait(barrier, ngx + ngy - 2)
-    for d in order:
-        halo_copy(0, d).start()
-    for i in range(rows):
-        ext[0][i] = v0[i].astype(BF16)
-
-    for c in range(parts_wide):
-        sketch_copy(c).wait()
+    for c in range(CHUNKS):
+        for d in order:
+            gather_outgoing(0, c, d)
+        if c == 0:
+            pl.semaphore_wait(barrier, ngx + ngy - 2)
+        for d in order:
+            halo_copy(0, c, d).start()
+    for c in range(CHUNKS):
         for i in range(rows):
-            high, low = split_bf16(sk[c, pl.ds(i, sk_rows, stride=rows), :])
-            shl[i, :, c * 128 : (c + 1) * 128] = jnp.concatenate([high, low], axis=0)
-    sketch_of(0)
+            ext[0][c][i] = v0[i, span(c), :].astype(BF16)
+
+    for n in range(parts_wide):
+        sketch_copy(n).wait()
+        for i in range(rows):
+            high, low = split_bf16(sk[n, pl.ds(i, sk_rows, stride=rows), :])
+            shl[i, :, n * 128 : (n + 1) * 128] = jnp.concatenate([high, low], axis=0)
+    for c in range(CHUNKS):
+        sketch_of(0, c)
+    keep_first(0)
 
     for s in range(STEPS):
-        for d in order:
-            halo_copy(s, d).wait_recv()
-
-        def row(i, carry):
-            if s == 0:
-                block_copy(i).wait()
-            parts = [ext[s][i]]
-            for k in range(1, slots):
-                parts.append(ext[s][jnp.where(k < live[i], cols[i, k], zero_slot)])
-            product = jnp.dot(
-                jnp.concatenate(parts, axis=1), blk[i], preferred_element_type=F32
-            )
-            vecs[s, i] = product
+        for c in range(CHUNKS):
+            for d in order:
+                halo_copy(s, c, d).wait_recv()
+
+            def row(i):
+                parts = [ext[s][c][i]]
+                for k in range(1, slots):
+                    index = jnp.where(k < live[i], cols[i, k], zero_slot)
+                    parts.append(ext[s][c][index])
+                product = jnp.dot(
+                    jnp.concatenate(parts, axis=1), blk[i], preferred_element_type=F32
+                )
+                vecs[s, i, span(c), :] = product
+                if s + 1 < STEPS:
+                    ext[s + 1][c][i] = product.astype(BF16)
+
+            def several(n, carry):
+                if s == 0 and c == 0:
+                    for u in range(UNROLL):
+                        block_copy(n * UNROLL + u).wait()
+                for u in range(UNROLL):
+                    row(n * UNROLL + u)
+                return carry
+
+            lax.fori_loop(0, rows // UNROLL, several, 0)
             if s + 1 < STEPS:
-                ext[s + 1][i] = product.astype(BF16)
-            return carry
-
-        lax.fori_loop(0, rows, row, 0)
-        if s + 1 < STEPS:
-            for d in order:
-                gather_outgoing(s + 1, d)
-                halo_copy(s + 1, d).start()
-        sketch_of(s + 1)
-        finish_gy(s)
-        if s > 0:
-            finish_gx(s - 1)
-
-    finish_gx(STEPS - 1)
-    finish_gy(STEPS)
-    finish_gx(STEPS)
+                for d in order:
+                    gather_outgoing(s + 1, c, d)
+                    halo_copy(s + 1, c, d).start()
+            sketch_of(s + 1, c)
+        if s % 2 == 0:
+            send_pair(s // 2)
+        else:
+            keep_first((s + 1) // 2)
+            finish_gy(0)
+
+    finish_gx(0)
+    finish_gy(1)
+    finish_gx(1)
     fbuf[h] = state["fac"]
     for delta in range(1, ngy):
         p3_copy(delta).start()
@@ -265,9 +302,10 @@
         fac_out[c * chunk : (c + 1) * chunk, :] = fbuf[c]
 
     for s in range(STEPS):
-        for d in order:
-            halo_copy(s, d).wait_send()
-    for s in range(STEPS + 1):
+        for c in range(CHUNKS):
+            for d in order:
+                halo_copy(s, c, d).wait_send()
+    for s in range((STEPS + 1) // 2):
         for delta in range(1, ngy):
             p1_copy(s, delta).wait_send()
         for delta in range(1, ngx):
@@ -329,6 +367,7 @@
     directions, send_count = send_rows.shape[1:]
     chunk = rhs // ngy
     count = STEPS + 1
+    pairs = count // 2
     places = rows + directions * send_count + 1
     hbm = pl.BlockSpec(memory_space=pltpu.HBM)
     vmem = pl.BlockSpec(memory_space=pltpu.VMEM)
@@ -350,23 +389,29 @@
             pltpu.VMEM((rows, rhs, width), F32),
             pltpu.VMEM((width // 128, sk_rows * rows, 128), F32),
             pltpu.VMEM((rows, 2 * sk_rows, width), BF16),
-            *[pltpu.VMEM((places, rhs, width), BF16) for step in range(STEPS)],
-            pltpu.VMEM((STEPS, directions, send_count, rhs, width), BF16),
-            pltpu.VMEM((count, ngy, chunk, 2 * sk_rows), F32),
-            pltpu.VMEM((count, ngy - 1, chunk, 2 * sk_rows), F32),
-            pltpu.VMEM((count, ngx, chunk, 2 * sk_rows), F32),
+            pltpu.VMEM(
+                (STEPS, CHUNKS, directions, send_count, rhs // CHUNKS, width), BF16
+            ),
+            pltpu.VMEM((pairs, rhs, sk_rows), F32),
+            pltpu.VMEM((pairs, ngy, chunk, 2 * sk_rows), F32),
+            pltpu.VMEM((pairs, ngy - 1, chunk, 2 * sk_rows), F32),
+            pltpu.VMEM((pairs, ngx, chunk, 2 * sk_rows), F32),
             pltpu.VMEM((ngy, chunk, 128), F32),
             dma((3,)),
             dma((1 + width // 128,)),
             dma((rows,)),
-            dma((STEPS, directions)),
-            dma((STEPS, directions)),
-            dma((count, ngy - 1)),
-            dma((count, ngy - 1)),
-            dma((count, ngx - 1)),
-            dma((count, ngx - 1)),
+            dma((STEPS, CHUNKS, directions)),
+            dma((STEPS, CHUNKS, directions)),
+            dma((pairs, ngy - 1)),
+            dma((pairs, ngy - 1)),
+            dma((pairs, ngx - 1)),
+            dma((pairs, ngx - 1)),
             dma((ngy - 1,)),
             dma((ngy - 1,)),
+            *[
+                pltpu.VMEM((places, rhs // CHUNKS, width), BF16)
+                for half in range(STEPS * CHUNKS)
+            ],
         ],
         compiler_params=pltpu.CompilerParams(
             collective_id=0, has_side_effects=True, vmem_limit_bytes=40 * 1024 * 1024

time: 51.4 us -> 44.7 us (0.87)
  Pallas kernels: 50.6 us -> 43.9 us
    pallas_call x1, Pallas kernels: 48.2 us -> 41.5 us  [on_device(): pl.pallas_call(functools.partial(power_kernel, ngx, ngy), name='power', o...]
where the time goes in v2:
time: 44.7 us; the launch traced here: 44.5 us
  Pallas kernels  43.9 us (98%)
  between operations  0.66 us (1%)
    pallas_call x1, Pallas kernels, on_device(): pl.pallas_call(functools.partial(power_kernel, ngx, ngy), name='power', o...  41.5 us
    pallas_call x1, Pallas kernels, on_device(): pl.pallas_call(basis_kernel, name='basis', out_shape=[jax.ShapeDtypeStruc...  2.37 us

profile of v2, /device:TPU:0, one launch (start us, length us, event | category | flops | bytes accessed | tf_op | source)
XLA Modules:
  0.0 44.5 jit_solution(996929977479269103)
XLA Ops:
  0.6 0.0 copy-start
  0.6 41.5 %power.1 = (f32[3,8,64,256]{3,2,1,0:T(8,128)S(1)}, f32[64,128]{1,0:T(8,128)S(1)}) custom-call(s32[8,8]{1,0:T(8,128)} %cols_hbm.1, s32[8]{0:T(128)} %live_hbm.1, s32[4,4]{1,0:T(4,128)} %bitcast.5, bf16[8,2048,256]{2,1,0:T(8,128)(2,1)} %bitcast.3, f32[8,64,256]{2,1,0:T(8,128)} %start.1, f32[512,256]{1,0:T(8,128)} %bitcast.4), custom_call_target="tpu_custom_call" | custom-call | tf_op jit(solution)/shard_map/power/pallas_call | solution.py:375
  42.1 0.0 copy-done
  42.1 2.4 %basis.1 = (f32[4,8,64,256]{3,2,1,0:T(8,128)}, f32[4,4,64]{2,1,0:T(4,128)}) custom-call(f32[8,64,256]{2,1,0:T(8,128)S(1)} %copy-done, f32[3,8,64,256]{3,2,1,0:T(8,128)S(1)} %get-tuple-element.4.vecs, f32[64,128]{1,0:T(8,128)S(1)} %get-tuple-element.5.fac), custom_call_target="tpu_custom_call" | custom-call | tf_op jit(solution)/shard_map/basis/pallas_call | solution.py:432
Async XLA Ops:
  0.6 41.5 %copy-start = (f32[8,64,256]{2,1,0:T(8,128)S(1)}, f32[8,64,256]{2,1,0:T(8,128)}, u32[]{:S(2)}) copy-start(f32[8,64,256]{2,1,0:T(8,128)} %start.1) | copy-start | bytes 1572868

commit v3 on v2

--- a/solution.py
+++ b/solution.py
@@ -228,17 +228,20 @@
             square = jnp.sum(residue * residue, axis=1, keepdims=True)
             length = jnp.sqrt(square + 1e-06)
             put(s, s, length)
-            units.append(residue / length)
+            if s < STEPS:
+                units.append(residue / length)
 
     for load in scalar_loads:
         load.wait()
     load_start.wait()
     for c in range(CHUNKS):
-        for d in order:
-            gather_outgoing(0, c, d)
         if c == 0:
+            for d in order:
+                gather_outgoing(0, c, d)
             pl.semaphore_wait(barrier, ngx + ngy - 2)
         for d in order:
+            if c > 0:
+                gather_outgoing(0, c, d)
             halo_copy(0, c, d).start()
     for c in range(CHUNKS):
         for i in range(rows):

time: 44.7 us -> 44.7 us (level)
  no operation moved by 1% of the time
where the time goes in v3:
time: 44.7 us; the launch traced here: 44.5 us
  Pallas kernels  43.9 us (98%)
  between operations  0.66 us (1%)
    pallas_call x1, Pallas kernels, on_device(): pl.pallas_call(functools.partial(power_kernel, ngx, ngy), name='power', o...  41.5 us
    pallas_call x1, Pallas kernels, on_device(): pl.pallas_call(basis_kernel, name='basis', out_shape=[jax.ShapeDtypeStruc...  2.37 us

profile of v3, /device:TPU:0, one launch (start us, length us, event | category | flops | bytes accessed | tf_op | source)
XLA Modules:
  0.0 44.5 jit_solution(16190351127410989703)
XLA Ops:
  0.6 0.0 copy-start
  0.6 41.5 %power.1 = (f32[3,8,64,256]{3,2,1,0:T(8,128)S(1)}, f32[64,128]{1,0:T(8,128)S(1)}) custom-call(s32[8,8]{1,0:T(8,128)} %cols_hbm.1, s32[8]{0:T(128)} %live_hbm.1, s32[4,4]{1,0:T(4,128)} %bitcast.5, bf16[8,2048,256]{2,1,0:T(8,128)(2,1)} %bitcast.3, f32[8,64,256]{2,1,0:T(8,128)} %start.1, f32[512,256]{1,0:T(8,128)} %bitcast.4), custom_call_target="tpu_custom_call" | custom-call | tf_op jit(solution)/shard_map/power/pallas_call | solution.py:378
  42.1 0.0 copy-done
  42.2 2.4 %basis.1 = (f32[4,8,64,256]{3,2,1,0:T(8,128)}, f32[4,4,64]{2,1,0:T(4,128)}) custom-call(f32[8,64,256]{2,1,0:T(8,128)S(1)} %copy-done, f32[3,8,64,256]{3,2,1,0:T(8,128)S(1)} %get-tuple-element.4.vecs, f32[64,128]{1,0:T(8,128)S(1)} %get-tuple-element.5.fac), custom_call_target="tpu_custom_call" | custom-call | tf_op jit(solution)/shard_map/basis/pallas_call | solution.py:435
Async XLA Ops:
  0.6 41.5 %copy-start = (f32[8,64,256]{2,1,0:T(8,128)S(1)}, f32[8,64,256]{2,1,0:T(8,128)}, u32[]{:S(2)}) copy-start(f32[8,64,256]{2,1,0:T(8,128)} %start.1) | copy-start | bytes 1572868
